TPU v7x, 32 devices: a whole 2x2x4 slice. The times are simulated.
32 devices in a mesh: gx: 4 (over y, x), gz: 8 (over z, core).
Axes of the slice: x: 2, y: 2, z: 4, core: 2. Of those that a mesh axis runs over, the one named last changes fastest.
Arguments:
- high_u: bfloat16 [128, 256, 512], P('gx', 'gz'), may hold values from -6 to 6
- high_v: bfloat16 [128, 256, 512], P('gx', 'gz'), may hold values from -6 to 6
- low_u: bfloat16 [512, 512], P(('gx', 'gz')), may hold values from -0.5 to 0.5
- low_v: bfloat16 [512, 512], P(('gx', 'gz')), may hold values from -0.5 to 0.5
- low_kx: int32 [512], P(('gx', 'gz')), may hold values from 0 to 64, as said below
- low_kz: int32 [512], P(('gx', 'gz')), may hold values from 0 to 64, as said below
- tau_inverse: bfloat16 [512, 512, 512], P(('gx', 'gz')), may hold values from -0.25 to 0.25
Outputs:
- high_term: bfloat16 [128, 256, 512], P('gx', 'gz')
- low_response: float32 [512, 512], P(('gx', 'gz'))
Inputs may be any that keep to these rules, and one draw needn't show every extreme that they name: Slot m holds the retained mode (low_kx[m], low_kz[m]); no two slots hold the same pair; the device that holds slot m owns that mode. `low_kz`: paired with low_kx slot by slot.
All inputs are finite; a program needn't handle non-finite values.
Results may differ from a plain program's by a relative error of at most 0.0047.
Values may be sent and summed in bfloat16 or wider, within the bound.
A program may use at most 128 MiB of HBM per device.

v0:
```python
import math

import jax
import jax.numpy as jnp
from jax import lax
from jax.sharding import PartitionSpec as P

KL = 32


CONTRACT_FIRST = (((0,), (0,)), ((), ()))


def axis_table(index, positions, length):
    wavenum = jnp.where(index <= KL, index, index - KL)
    phases = wavenum[:, None] * positions[None, :] % length
    angles = phases.astype(jnp.float32) * (2.0 * math.pi / length)
    return jnp.where((index <= KL)[:, None], jnp.cos(angles), jnp.sin(angles))


def mode_weight(index_x, index_z):
    return jnp.where(index_x > 0, 2.0, 1.0).astype(jnp.float32) * jnp.where(
        index_z > 0, 2.0, 1.0
    ).astype(jnp.float32)


def on_device(high_u, high_v, low_u, low_v, low_kx, low_kz, tau_inverse):
    cells_x, cells_z, levels = high_u.shape
    owned_modes = low_u.shape[0]
    groups_x = lax.axis_size("gx")
    groups_z = lax.axis_size("gz")
    length_x = groups_x * cells_x
    length_z = groups_z * cells_z
    points = cells_x * cells_z
    unitary = 1.0 / math.sqrt(length_x * length_z)
    where_x = lax.axis_index("gx") * cells_x + jnp.arange(cells_x, dtype=jnp.int32)
    where_z = lax.axis_index("gz") * cells_z + jnp.arange(cells_z, dtype=jnp.int32)

    def patterns(index_x, index_z):
        table_x = axis_table(index_x, where_x, length_x)
        table_z = axis_table(index_z, where_z, length_z)
        return (
            (table_x[:, :, None] * table_z[:, None, :])
            .reshape(index_x.shape[0], points)
            .astype(jnp.bfloat16)
        )

    shard_u = lax.all_gather(low_u, ("gx", "gz"), axis=0, tiled=True)
    shard_v = lax.all_gather(low_v, ("gx", "gz"), axis=0, tiled=True)
    shard_x = lax.all_gather(low_kx.astype(jnp.bfloat16), ("gx", "gz"), axis=0, tiled=True)
    shard_z = lax.all_gather(low_kz.astype(jnp.bfloat16), ("gx", "gz"), axis=0, tiled=True)
    index_x = shard_x.astype(jnp.int32)
    index_z = shard_z.astype(jnp.int32)
    stacked = jnp.concatenate([shard_u, shard_v], axis=1)
    coarse = lax.dot_general(
        patterns(index_x, index_z), stacked, CONTRACT_FIRST, preferred_element_type=jnp.float32
    )
    add_every_x = index_x
    add_every_z = index_z
    coarse, every_x, every_z = (coarse, add_every_x, add_every_z)
    fine_u = high_u.reshape(points, levels)
    fine_v = high_v.reshape(points, levels)
    coarse_u = coarse[:, :levels]
    coarse_v = coarse[:, levels:]
    self_term = (coarse_u * coarse_v + fine_u.astype(jnp.float32) * fine_v).astype(jnp.bfloat16)
    cross_term = coarse_u * fine_v + fine_u * coarse_v
    cross_round = cross_term.astype(jnp.bfloat16)
    own_weight = mode_weight(low_kx, low_kz)[:, None]
    products = jnp.concatenate([self_term, cross_round], axis=1)
    serial = jnp.arange(owned_modes * groups_x * lax.axis_size("gz"), dtype=jnp.int32)
    column = serial // (owned_modes * groups_x)
    row_group = serial // owned_modes % groups_x
    modes = (row_group * groups_z + column) * owned_modes + serial % owned_modes
    table = patterns(jnp.take(every_x, modes), jnp.take(every_z, modes))
    column_part = lax.psum_scatter(
        jnp.dot(table, products, preferred_element_type=jnp.float32) * unitary,
        "gz",
        scatter_dimension=0,
        tiled=True,
    )
    totals = lax.psum_scatter(column_part, "gx", scatter_dimension=0, tiled=True)
    forcing = totals[:, :levels]
    cross_low = (own_weight * totals[:, levels:]).astype(jnp.bfloat16)
    index_x = every_x
    index_z = every_z
    restored = lax.dot_general(
        patterns(index_x, index_z),
        lax.all_gather(cross_low, ("gx", "gz"), axis=0, tiled=True),
        CONTRACT_FIRST,
        preferred_element_type=jnp.float32,
    )
    high_term = (
        (cross_term - unitary * restored).astype(jnp.bfloat16).reshape(cells_x, cells_z, levels)
    )
    low_response = jnp.einsum(
        "mij,mj->mi", tau_inverse, forcing.astype(jnp.bfloat16), preferred_element_type=jnp.float32
    )
    return (high_term, low_response)


def solution(mesh):
    placed = (
        P("gx", "gz", None),
        P("gx", "gz", None),
        P(("gx", "gz"), None),
        P(("gx", "gz"), None),
        P(("gx", "gz")),
        P(("gx", "gz")),
        P(("gx", "gz"), None, None),
    )
    return jax.shard_map(
        on_device,
        mesh=mesh,
        in_specs=placed,
        out_specs=(P("gx", "gz", None), P(("gx", "gz"), None)),
        check_vma=False,
    )
```

profile of v0, /device:TPU:1, one launch (start us, length us, event | category | flops | bytes accessed | tf_op | source)
XLA Modules:
  0.0 265.2 jit_solution(10418261134492784979)
XLA Ops:
  7.2 0.0 reduce-scatter.3.cloned.1.call-start
  7.2 0.7 convert_element_type.82
  7.9 0.7 convert_element_type.85
  8.5 0.2 dynamic-update-slice
  8.7 0.2 dynamic-update-slice.1
  9.0 40.5 %all-reduce.2 = (bf16[512]{0:T(512)(128)(2,1)S(1)}, bf16[512]{0:T(512)(128)(2,1)S(1)}) all-reduce(bf16[512]{0:T(512)(128)(2,1)S(1)} %dynamic-update-slice.1, bf16[512]{0:T(512)(128)(2,1)S(1)} %dynamic-update-slice), channel_id=1, replica_groups=mesh['gx'=4,'gz'=8] {'gx','gz'}, use_global_device_ids=true, to_apply=%add.1 | all-reduce | flops 1024 | bytes 4096
  49.5 0.0 copy-start.2
  49.5 0.0 copy-start.3
  49.6 3.5 %gather_fusion = s32[512]{0:T(512)S(1)} fusion(s32[512]{0:T(512)S(1)} %convert_element_type.83, s32[1024]{0:T(1024)S(1)} %pad_clamp_fusion), kind=kCustom, calls=%fused_computation.clone | custom fusion | bytes 6144 | tf_op jit(solution)/shard_map/jit(_take)/gather | solution.py:74
  53.1 3.5 %gather_fusion.1 = s32[512]{0:T(512)S(1)} fusion(s32[512]{0:T(512)S(1)} %convert_element_type.86, s32[1024]{0:T(1024)S(1)} %pad_clamp_fusion), kind=kCustom, calls=%fused_computation.1.clone | custom fusion | bytes 6144 | tf_op jit(solution)/shard_map/jit(_take)/gather | solution.py:74
  56.7 0.0 copy-done.2
  56.7 43.6 %all_gather.17 = bf16[512,512]{1,0:T(8,128)(2,1)S(1)} all-gather(bf16[16,512]{1,0:T(8,128)(2,1)S(1)} %copy-done.2), channel_id=1, replica_groups=mesh['gx'=4,'gz'=8] {'gx','gz'}, dimensions={0}, use_global_device_ids=true | all-gather | bytes 540672 | tf_op jit(solution)/shard_map/all_gather | solution.py:48
  100.3 0.0 copy-done.3
  100.3 38.9 %all_gather.18 = bf16[512,512]{1,0:T(8,128)(2,1)S(1)} all-gather(bf16[16,512]{1,0:T(8,128)(2,1)S(1)} %copy-done.3), channel_id=1, replica_groups=mesh['gx'=4,'gz'=8] {'gx','gz'}, dimensions={0}, use_global_device_ids=true | all-gather | bytes 540672 | tf_op jit(solution)/shard_map/all_gather | solution.py:49
  139.2 0.6 sine_select_fusion.1
  139.8 0.6 sine_select_fusion
  140.4 0.3 multiply_convert_fusion.1
  140.7 0.3 multiply_convert_fusion
  140.9 0.0 copy-start
  140.9 0.0 copy-start.1
  141.0 1.3 fusion.10
  142.2 0.0 copy-done
  142.2 0.3 copy-done.1
  142.5 1.1 fusion.46
  143.6 2.6 fusion.7
  146.2 0.0 copy-start.4
  146.2 0.0 copy-start.5
  146.2 0.0 reduce-scatter.3.cloned.1.call-update
  146.2 0.0 reduce-scatter.5.cloned.1.call-start
  146.2 31.1 %reduce-scatter.3.cloned.1.call-done = f32[64,1024]{1,0:T(8,128)} async-done(((f32[512,1024]{1,0:T(8,128)}), f32[64,1024]{1,0:T(8,128)}) %reduce-scatter.3.cloned.1.call-update) | async-done | bytes 262160 | tf_op jit(solution)/shard_map/reduce_scatter | solution.py:75
  177.3 0.0 reduce-scatter.5.cloned.1.call-update
  177.3 0.0 copy-done.4
  177.3 0.0 copy-done.5
  177.4 27.7 %reduce-scatter.5.cloned.1.call-done = f32[16,1024]{1,0:T(8,128)} async-done(((f32[64,1024]{1,0:T(8,128)}), f32[16,1024]{1,0:T(8,128)}) %reduce-scatter.5.cloned.1.call-update) | async-done | bytes 65552 | tf_op jit(solution)/shard_map/reduce_scatter | solution.py:81
  205.1 0.8 fusion.26
  205.9 43.7 %all_gather.19 = bf16[512,512]{1,0:T(8,128)(2,1)S(1)} all-gather(bf16[16,512]{1,0:T(8,128)(2,1)S(1)} %fusion.26), channel_id=1, replica_groups=mesh['gx'=4,'gz'=8] {'gx','gz'}, dimensions={0}, use_global_device_ids=true | all-gather | bytes 540672 | tf_op jit(solution)/shard_map/all_gather | solution.py:88
  249.6 0.8 fusion.29
  250.4 5.6 %fusion.27 = f32[16,1,512]{2,1,0:T(1,128)S(1)} fusion(bf16[16,512,512]{2,1,0:T(8,128)(2,1)} %param.15, bf16[16,512,1]{1,0,2:T(8,128)(2,1)S(1)} %fusion.29), kind=kOutput, calls=%fused_computation.60 | convolution fusion | flops 8388608 | bytes 8437760 | tf_op jit(solution)/shard_map/mij,mj->mi/dot_general | solution.py:95
  256.0 0.6 copy.14
  256.6 1.7 subtract_convert_fusion
  (15 shorter events, 0.1 us)
Async XLA Ops:
  7.2 170.2 %reduce-scatter.3.cloned.1.call-start = ((), (), s32[]{:S(2)}) async-start(), calls=%async_computation.2 | async-start | bytes 2359296 | tf_op jit(solution)/shard_map/reduce_scatter | solution.py:75
  49.5 7.1 %copy-start.2 = (bf16[16,512]{1,0:T(8,128)(2,1)S(1)}, bf16[16,512]{1,0:T(8,128)(2,1)}, u32[]{:S(2)}) copy-start(bf16[16,512]{1,0:T(8,128)(2,1)} %param.11) | copy-start | bytes 49156
  49.5 50.8 %copy-start.3 = (bf16[16,512]{1,0:T(8,128)(2,1)S(1)}, bf16[16,512]{1,0:T(8,128)(2,1)}, u32[]{:S(2)}) copy-start(bf16[16,512]{1,0:T(8,128)(2,1)} %param.12) | copy-start | bytes 49156
  140.9 1.3 copy-start
  140.9 1.5 copy-start.1
  146.2 31.2 %copy-start.4 = (s32[16]{0:T(128)S(1)}, s32[16]{0:T(128)}, u32[]{:S(2)}) copy-start(s32[16]{0:T(128)} %param.14) | copy-start | bytes 196
  146.2 31.2 %copy-start.5 = (s32[16]{0:T(128)S(1)}, s32[16]{0:T(128)}, u32[]{:S(2)}) copy-start(s32[16]{0:T(128)} %param.13) | copy-start | bytes 196
  146.2 58.9 %reduce-scatter.5.cloned.1.call-start = ((), (), s32[]{:S(2)}) async-start(), calls=%async_computation.3 | async-start | bytes 327680 | tf_op jit(solution)/shard_map/reduce_scatter | solution.py:81
Sparse Core Ops, SparseCore 0:
  146.3 30.9 reduce-scatter.2
  180.1 24.9 reduce-scatter.4
where the time goes:
time: 266 us; the launch traced here: 265 us
  blocking collectives  167 us (63%)
  waiting for transfers between devices  58.8 us (22%)
  between operations  14.2 us (5%)
  matrix products  11.2 us (4%)
  local copies, waits for them, and re-layouts  9.08 us (3%)
  other arithmetic  5.06 us (2%)
    all_gather x1, blocking collectives, on_device(): lax.all_gather(cross_low, ('gx', 'gz'), axis=0, tiled=True)  43.7 us
    all_gather x1, blocking collectives, on_device(): shard_u = lax.all_gather(low_u, ('gx', 'gz'), axis=0, tiled=True)  43.6 us
    unnamed x1, blocking collectives  40.5 us
    all_gather x1, blocking collectives, on_device(): shard_v = lax.all_gather(low_v, ('gx', 'gz'), axis=0, tiled=True)  38.9 us
    reduce_scatter x1, waiting for transfers between devices, on_device(): lax.psum_scatter(jnp.dot(table, products, preferred_element_type=jnp.floa...  31.1 us
    reduce_scatter x1, waiting for transfers between devices, on_device(): lax.psum_scatter(column_part, 'gx', scatter_dimension=0, tiled=True)  27.7 us
    gather x2, local copies, waits for them, and re-layouts, on_device(): table = patterns(jnp.take(every_x, modes), jnp.take(every_z, modes))  6.98 us
    dot_general x1, matrix products, on_device(): jnp.einsum('mij,mj->mi', tau_inverse, forcing.astype(jnp.bfloat16), prefe...  5.63 us
  transfers between devices with their start and end apart: 2, of which 2 were waited for; matrix products, arithmetic and copies ran while one was open for 0% of the time, Pallas kernels for 0%

commit v1 on v0

v1 whole, which is shorter than its diff:
```python
import math

import jax
import jax.numpy as jnp
from jax import lax
from jax.experimental import pallas as pl
from jax.experimental.pallas import tpu as pltpu
from jax.sharding import PartitionSpec as P

KL = 32
LANES = 128
MESH = pl.DeviceIdType.MESH


CONTRACT_FIRST = (((0,), (0,)), ((), ()))


def axis_table(index, positions, length):
    wavenum = jnp.where(index <= KL, index, index - KL)
    phases = wavenum[:, None] * positions[None, :] % length
    angles = phases.astype(jnp.float32) * (2.0 * math.pi / length)
    return jnp.where((index <= KL)[:, None], jnp.cos(angles), jnp.sin(angles))


def mode_weight(index_x, index_z):
    return jnp.where(index_x > 0, 2.0, 1.0).astype(jnp.float32) * jnp.where(
        index_z > 0, 2.0, 1.0
    ).astype(jnp.float32)


def copy_to(src, dst, send, recv, device):
    return pltpu.make_async_remote_copy(
        src_ref=src, dst_ref=dst, send_sem=send, recv_sem=recv, device_id=device, device_id_type=MESH
    )


class Place:
    def __init__(self, groups_x, groups_z):
        self.nx, self.nc = groups_x, groups_z // 2
        self.g = lax.axis_index("gx")
        gz = lax.axis_index("gz")
        self.gz = gz
        self.c, self.k = gz // 2, gz % 2

    def partner(self):
        return (self.g, 2 * self.c + 1 - self.k)

    def along_x(self, i):
        return lax.rem(self.g + i, self.nx)

    def along_c(self, j):
        return lax.rem(self.c + j, self.nc)


def greet(p):
    barrier = pltpu.get_barrier_semaphore()
    pl.semaphore_signal(barrier, inc=1, device_id=p.partner(), device_id_type=MESH)

    @pl.loop(1, p.nx)
    def _(i):
        pl.semaphore_signal(barrier, inc=1, device_id=(p.along_x(i), p.gz), device_id_type=MESH)

    @pl.loop(1, p.nc)
    def _(j):
        pl.semaphore_signal(
            barrier, inc=1, device_id=(p.g, 2 * p.along_c(j) + p.k), device_id_type=MESH
        )

    pl.semaphore_wait(barrier, 1 + p.nx - 1 + p.nc - 1)


def gather_kernel(groups_x, groups_z, own, out, local_sem, send_x, send_c, send_p, recv):
    p = Place(groups_x, groups_z)
    greet(p)
    other = p.partner()

    def to_x(i, c, src):
        gz = 2 * c + p.k
        return copy_to(src, out.at[p.g, gz], send_x.at[i, c], recv.at[p.g, gz], (p.along_x(i), p.gz))

    def to_c(j, src):
        return copy_to(
            src, out.at[p.g, p.gz], send_c.at[j], recv.at[p.g, p.gz], (p.g, 2 * p.along_c(j) + p.k)
        )

    def to_p(g, c, src):
        gz = 2 * c + p.k
        return copy_to(src, out.at[g, gz], send_p.at[g, c], recv.at[g, gz], other)

    def arrived(g, gz):
        copy_to(own, out.at[g, gz], send_c.at[0], recv.at[g, gz], other).wait_recv()

    @pl.loop(1, p.nc)
    def _(j):
        to_c(j, own).start()

    @pl.loop(1, p.nx)
    def _(i):
        to_x(i, p.c, own).start()

    to_p(p.g, p.c, own).start()
    keep = pltpu.make_async_copy(own, out.at[p.g, p.gz], local_sem)
    keep.start()

    @pl.loop(1, p.nc)
    def _(j):
        c = p.along_c(j)
        arrived(p.g, 2 * c + p.k)

        @pl.loop(1, p.nx)
        def _(i):
            to_x(i, c, out.at[p.g, 2 * c + p.k]).start()

        to_p(p.g, c, out.at[p.g, 2 * c + p.k]).start()

    @pl.loop(0, p.nc)
    def _(j):
        c = p.along_c(j)

        @pl.loop(1, p.nx)
        def _(i):
            g = p.along_x(i)
            arrived(g, 2 * c + p.k)
            to_p(g, c, out.at[g, 2 * c + p.k]).start()

    @pl.loop(0, p.nx)
    def _(g):
        @pl.loop(0, p.nc)
        def _(c):
            arrived(g, 2 * c + 1 - p.k)

    keep.wait()

    @pl.loop(1, p.nc)
    def _(j):
        to_c(j, own).wait_send()

    @pl.loop(0, p.nc)
    def _(c):
        @pl.loop(1, p.nx)
        def _(i):
            to_x(i, c, own).wait_send()

        @pl.loop(0, p.nx)
        def _(g):
            to_p(g, c, own).wait_send()


def gather_all(block, collective_id):
    groups_x, groups_z = lax.axis_size("gx"), lax.axis_size("gz")
    rows, columns = block.shape
    chips = groups_z // 2
    dma = pltpu.SemaphoreType.DMA

    def body(*refs):
        gather_kernel(groups_x, groups_z, *refs)

    return pl.pallas_call(
        body,
        out_shape=jax.ShapeDtypeStruct((groups_x, groups_z, rows, columns), block.dtype),
        in_specs=[pl.BlockSpec(memory_space=pltpu.VMEM)],
        out_specs=pl.BlockSpec(memory_space=pltpu.VMEM),
        scratch_shapes=[
            dma,
            dma((groups_x, chips)),
            dma((chips,)),
            dma((groups_x, chips)),
            dma((groups_x, groups_z)),
        ],
        compiler_params=pltpu.CompilerParams(collective_id=collective_id, has_side_effects=True),
        name="gather",
    )(block).reshape(groups_x * groups_z * rows, columns)


def scatter_kernel(
    groups_x, groups_z, part, out, pair, sums, from_x, acc, sent_c, from_c,
    send_p, recv_p, send_x, recv_x, send_c, recv_c,
):
    p = Place(groups_x, groups_z)
    greet(p)
    other = p.partner()

    def to_p(g):
        return copy_to(part.at[g, :, 1 - p.k], pair.at[g], send_p.at[g], recv_p.at[g], other)

    def to_x(i):
        g = p.along_x(i)
        return copy_to(sums.at[g], from_x.at[p.g], send_x.at[g], recv_x.at[p.g], (g, p.gz))

    def to_c(j):
        c = p.along_c(j)
        return copy_to(sent_c.at[c], from_c.at[p.c], send_c.at[c], recv_c.at[p.c], (p.g, 2 * c + p.k))

    @pl.loop(1, p.nx + 1)
    def _(i):
        to_p(p.along_x(i)).start()

    def chip_sum(g):
        to_p(g).wait_recv()
        return part[g, :, p.k].astype(jnp.float32) + pair[g].astype(jnp.float32)

    @pl.loop(1, p.nx)
    def _(i):
        g = p.along_x(i)
        sums[g] = chip_sum(g).astype(sums.dtype)
        to_x(i).start()

    acc[...] = chip_sum(p.g)

    @pl.loop(1, p.nx)
    def _(i):
        g = p.along_x(i)
        copy_to(sums.at[g], from_x.at[g], send_x.at[g], recv_x.at[g], other).wait_recv()
        acc[...] += from_x[g].astype(jnp.float32)

    @pl.loop(1, p.nc)
    def _(j):
        c = p.along_c(j)
        sent_c[c] = acc[c].astype(sent_c.dtype)
        to_c(j).start()

    out[...] = acc[p.c]

    @pl.loop(1, p.nc)
    def _(j):
        c = p.along_c(j)
        copy_to(sent_c.at[c], from_c.at[c], send_c.at[c], recv_c.at[c], other).wait_recv()
        out[...] += from_c[c].astype(jnp.float32)

    @pl.loop(0, p.nx)
    def _(g):
        to_p(g).wait_send()

    @pl.loop(1, p.nx)
    def _(i):
        to_x(i).wait_send()

    @pl.loop(1, p.nc)
    def _(j):
        to_c(j).wait_send()


def scatter_sum(part, collective_id):
    groups_x, groups_z = lax.axis_size("gx"), lax.axis_size("gz")
    modes, columns = part.shape
    rows = modes // (groups_x * groups_z)
    chips = groups_z // 2
    dma = pltpu.SemaphoreType.DMA
    kind = part.dtype

    def body(*refs):
        scatter_kernel(groups_x, groups_z, *refs)

    return pl.pallas_call(
        body,
        out_shape=jax.ShapeDtypeStruct((rows, columns), jnp.float32),
        in_specs=[pl.BlockSpec(memory_space=pltpu.VMEM)],
        out_specs=pl.BlockSpec(memory_space=pltpu.VMEM),
        scratch_shapes=[
            pltpu.VMEM((groups_x, chips, rows, columns), kind),
            pltpu.VMEM((groups_x, chips, rows, columns), kind),
            pltpu.VMEM((groups_x, chips, rows, columns), kind),
            pltpu.VMEM((chips, rows, columns), jnp.float32),
            pltpu.VMEM((chips, rows, columns), kind),
            pltpu.VMEM((chips, rows, columns), kind),
            dma((groups_x,)),
            dma((groups_x,)),
            dma((groups_x,)),
            dma((groups_x,)),
            dma((chips,)),
            dma((chips,)),
        ],
        compiler_params=pltpu.CompilerParams(collective_id=collective_id, has_side_effects=True),
        name="scatter",
    )(part.reshape(groups_x, chips, 2, rows, columns))


def on_device(high_u, high_v, low_u, low_v, low_kx, low_kz, tau_inverse):
    cells_x, cells_z, levels = high_u.shape
    groups_x = lax.axis_size("gx")
    groups_z = lax.axis_size("gz")
    length_x = groups_x * cells_x
    length_z = groups_z * cells_z
    points = cells_x * cells_z
    unitary = 1.0 / math.sqrt(length_x * length_z)
    where_x = lax.axis_index("gx") * cells_x + jnp.arange(cells_x, dtype=jnp.int32)
    where_z = lax.axis_index("gz") * cells_z + jnp.arange(cells_z, dtype=jnp.int32)

    lane = jnp.arange(LANES, dtype=jnp.int32)[None, :]
    labels = jnp.where(lane == 0, low_kx[:, None], low_kz[:, None]).astype(jnp.bfloat16)
    block = jnp.concatenate([low_u, low_v, labels], axis=1)
    every = gather_all(block, 0)
    index_x = every[:, 2 * levels].astype(jnp.int32)
    index_z = every[:, 2 * levels + 1].astype(jnp.int32)
    table_x = axis_table(index_x, where_x, length_x)
    table_z = axis_table(index_z, where_z, length_z)
    patterns = (
        (table_x[:, :, None] * table_z[:, None, :])
        .reshape(index_x.shape[0], points)
        .astype(jnp.bfloat16)
    )
    coarse = lax.dot_general(
        patterns, every[:, : 2 * levels], CONTRACT_FIRST, preferred_element_type=jnp.float32
    )
    fine_u = high_u.reshape(points, levels)
    fine_v = high_v.reshape(points, levels)
    coarse_u = coarse[:, :levels]
    coarse_v = coarse[:, levels:]
    self_term = (coarse_u * coarse_v + fine_u.astype(jnp.float32) * fine_v).astype(jnp.bfloat16)
    cross_term = coarse_u * fine_v + fine_u * coarse_v
    cross_round = cross_term.astype(jnp.bfloat16)
    products = jnp.concatenate([self_term, cross_round], axis=1)
    part = jnp.dot(patterns, products, preferred_element_type=jnp.float32) * unitary
    totals = scatter_sum(part.astype(jnp.bfloat16), 1)
    own_weight = mode_weight(low_kx, low_kz)[:, None]
    forcing = totals[:, :levels]
    cross_low = (own_weight * totals[:, levels:]).astype(jnp.bfloat16)
    restored = lax.dot_general(
        patterns, gather_all(cross_low, 2), CONTRACT_FIRST, preferred_element_type=jnp.float32
    )
    high_term = (
        (cross_term - unitary * restored).astype(jnp.bfloat16).reshape(cells_x, cells_z, levels)
    )
    low_response = jnp.einsum(
        "mij,mj->mi", tau_inverse, forcing.astype(jnp.bfloat16), preferred_element_type=jnp.float32
    )
    return (high_term, low_response)


def solution(mesh):
    placed = (
        P("gx", "gz", None),
        P("gx", "gz", None),
        P(("gx", "gz"), None),
        P(("gx", "gz"), None),
        P(("gx", "gz")),
        P(("gx", "gz")),
        P(("gx", "gz"), None, None),
    )
    return jax.shard_map(
        on_device,
        mesh=mesh,
        in_specs=placed,
        out_specs=(P("gx", "gz", None), P(("gx", "gz"), None)),
        check_vma=False,
    )
```

time: 266 us -> 70.7 us (0.27)
  blocking collectives: 167 us -> 0 us
  waiting for transfers between devices: 58.8 us -> 0 us
  Pallas kernels: 0 us -> 48.8 us
  between operations: 14.2 us -> 0.81 us
  local copies, waits for them, and re-layouts: 9.08 us -> 3.08 us
    all_gather x3 -> x0, blocking collectives: 126 us -> none  [the longest x1 43.7 us: on_device(): lax.all_gather(cross_low, ('gx', 'gz'), axis=0, tiled=True)]
    reduce_scatter x2 -> x0, waiting for transfers between devices: 58.8 us -> none  [the longest x1 31.1 us: on_device(): lax.psum_scatter(jnp.dot(table, products, preferred_element_type=jnp.floa...]
    pallas_call x0 -> x3, Pallas kernels: none -> 48.8 us  [the longest x2 32.7 us: gather_all(): pl.pallas_call(body, out_shape=jax.ShapeDtypeStruct((groups_x, groups_z,...]
    unnamed x1 -> x0, blocking collectives: 40.5 us -> none
    gather x2 -> x0, local copies, waits for them, and re-layouts: 6.98 us -> none  [on_device(): table = patterns(jnp.take(every_x, modes), jnp.take(every_z, modes))]
  transfers between devices with their start and end apart: 2 -> 0, of which waited for: 2 -> 0; matrix products, arithmetic and copies ran while one was open for 0% -> 0% of each run, Pallas kernels for 0% -> 0%
where the time goes in v1:
time: 70.7 us; the launch traced here: 70.1 us
  Pallas kernels  48.8 us (69%)
  matrix products  11.9 us (17%)
  other arithmetic  5.57 us (8%)
  local copies, waits for them, and re-layouts  3.08 us (4%)
  between operations  0.81 us (1%)
    pallas_call x2, Pallas kernels, gather_all(): pl.pallas_call(body, out_shape=jax.ShapeDtypeStruct((groups_x, groups_z,...  32.7 us
    pallas_call x1, Pallas kernels, scatter_sum(): pl.pallas_call(body, out_shape=jax.ShapeDtypeStruct((rows, columns), jnp....  16.1 us
    dot_general x1, matrix products, on_device(): jnp.einsum('mij,mj->mi', tau_inverse, forcing.astype(jnp.bfloat16), prefe...  5.63 us
    dot_general x1, matrix products, on_device(): lax.dot_general(patterns, gather_all(cross_low, 2), CONTRACT_FIRST, prefe...  2.72 us
    dot_general x1, matrix products, on_device(): jnp.dot(patterns, products, preferred_element_type=jnp.float32) * unitary  2.26 us
    convert_element_type x1, other arithmetic, on_device(): cross_low = (own_weight * totals[:, levels:]).astype(jnp.bfloat16)  1.44 us

profile of v1, /device:TPU:1, one launch (start us, length us, event | category | flops | bytes accessed | tf_op | source)
XLA Modules:
  0.0 70.1 jit_solution(1156151395962078251)
XLA Ops:
  0.6 0.7 %select_convert_fusion = bf16[16,128]{1,0:T(8,128)(2,1)S(1)} fusion(s32[16]{0:T(128)} %param.12, s32[16]{0:T(128)} %param.11, pred[128]{0:T(512)(128)(4,1)S(1)} %iota_compare_fusion), kind=kLoop, calls=%fused_computation.44 | loop fusion | flops 4096 | bytes 4352 | tf_op jit(solution)/shard_map/convert_element_type | solution.py:290
  1.4 1.4 %pad_maximum_fusion.refs_0_ = bf16[16,1152]{1,0:T(8,128)(2,1)} fusion(bf16[16,128]{1,0:T(8,128)(2,1)S(1)} %select_convert_fusion, bf16[16,512]{1,0:T(8,128)(2,1)} %param.10, bf16[16,512]{1,0:T(8,128)(2,1)} %param.9), kind=kLoop, calls=%fused_computation.33 | loop fusion | flops 110592 | bytes 73728 | tf_op jit(solution)/shard_map/concatenate | solution.py:291
  2.7 18.4 %gather.2 = bf16[4,8,16,1152]{3,2,1,0:T(8,128)(2,1)} custom-call(bf16[16,1152]{1,0:T(8,128)(2,1)} %pad_maximum_fusion.refs_0_), custom_call_target="tpu_custom_call" | custom-call | tf_op jit(solution)/shard_map/gather/pallas_call | solution.py:158
  21.1 0.0 copy-start
  21.1 1.2 %fusion.24 = (bf16[512,1]{1,0:T(8,128)(2,1)S(1)}, bf16[512,1]{1,0:T(8,128)(2,1)S(1)}) fusion(bf16[512,1152]{1,0:T(8,128)(2,1)} %bitcast.31), kind=kLoop, calls=%fused_computation.53 | loop fusion | bytes 4096 | tf_op jit(solution)/shard_map/slice | solution.py:293
  22.3 0.1 copy.13
  22.4 0.1 copy.14
  22.7 0.6 sine_select_fusion
  23.3 0.3 multiply_convert_fusion.1
  23.5 0.0 copy-done
  23.5 0.0 copy-start.1
  23.6 0.0 copy-start.2
  23.6 1.2 %fusion.9 = f32[1024,1024]{1,0:T(8,128)S(1)} fusion(bf16[512,1024]{0,1:T(8,128)(2,1)S(1)} %bitcast.27, bf16[512,1152]{1,0:T(8,128)(2,1)S(1)} %bitcast.32), kind=kOutput, calls=%fused_computation.13 | convolution fusion | flops 1073741824 | bytes 6291456 | tf_op jit(solution)/shard_map/dot_general | solution.py:302
  24.8 0.0 copy-done.1
  24.8 0.3 copy-done.2
  25.1 1.1 %fusion.22 = (bf16[1024,512]{1,0:T(8,128)(2,1)S(1)}, f32[1024,512]{1,0:T(8,128)S(1)}, bf16[1024,512]{1,0:T(8,128)(2,1)S(1)}) fusion(f32[1024,1024]{1,0:T(8,128)S(1)} %fusion.9, bf16[32,32,512]{2,1,0:T(8,128)(2,1)S(1)} %copy-done.1, bf16[32,32,512]{2,1,0:T(8,128)(2,1)S(1)} %copy-done.2), kind=kLoop, calls=%fused_computation.52 | loop fusion | flops 5242880 | bytes 10485760 | tf_op jit(solution)/shard_map/convert_element_type | solution.py:311
  26.2 0.0 copy-start.3
  26.2 0.0 copy-start.4
  26.2 2.3 %multiply_convert_fusion = bf16[512,1024]{1,0:T(8,128)(2,1)} fusion(bf16[512,1024]{0,1:T(8,128)(2,1)S(1)} %bitcast.28, bf16[1024,512]{1,0:T(8,128)(2,1)S(1)} %get-tuple-element.2, bf16[1024,512]{1,0:T(8,128)(2,1)S(1)} %get-tuple-element.4), kind=kOutput, calls=%fused_computation.11 | convolution fusion | flops 1078984704 | bytes 4194304 | tf_op jit(solution)/shard_map/dot_general | solution.py:313
  28.5 16.1 %scatter.1 = f32[16,1024]{1,0:T(8,128)} custom-call(bf16[4,4,2,16,1024]{4,3,2,1,0:T(8,128)(2,1)} %bitcast.33), custom_call_target="tpu_custom_call" | custom-call | tf_op jit(solution)/shard_map/scatter/pallas_call | solution.py:254
  44.5 0.0 copy-done.3
  44.5 0.0 copy-done.4
  44.6 1.4 %multiply_convert_fusion.2.refs_0_ = bf16[16,512]{1,0:T(8,128)(2,1)} fusion(f32[16,1024]{1,0:T(8,128)} %scatter.1, f32[16]{0:T(128)S(1)} %fusion.20), kind=kLoop, calls=%fused_computation.38 | loop fusion | flops 16384 | bytes 49216 | tf_op jit(solution)/shard_map/convert_element_type | solution.py:317
  46.0 14.3 %gather.3 = bf16[4,8,16,512]{3,2,1,0:T(8,128)(2,1)} custom-call(bf16[16,512]{1,0:T(8,128)(2,1)} %multiply_convert_fusion.2.refs_0_), custom_call_target="tpu_custom_call" | custom-call | tf_op jit(solution)/shard_map/gather/pallas_call | solution.py:158
  60.3 2.7 %subtract_convert_fusion = bf16[1024,512]{1,0:T(8,128)(2,1)} fusion(f32[1024,512]{1,0:T(8,128)S(1)} %get-tuple-element.3, bf16[512,1024]{0,1:T(8,128)(2,1)S(1)} %bitcast.29, bf16[512,512]{1,0:T(8,128)(2,1)} %bitcast.30), kind=kOutput, calls=%fused_computation.10 | convolution fusion | flops 538443776 | bytes 4718592 | tf_op jit(solution)/shard_map/dot_general | solution.py:318
  63.1 0.8 %fusion.19 = bf16[16,512,1]{1,0,2:T(8,128)(2,1)S(1)} fusion(f32[16,1024]{1,0:T(8,128)} %scatter.1), kind=kLoop, calls=%fused_computation.39 | loop fusion | bytes 32768 | tf_op jit(solution)/shard_map/slice | solution.py:316
  63.8 5.6 %fusion.17 = f32[16,1,512]{2,1,0:T(1,128)S(1)} fusion(bf16[16,512,512]{2,1,0:T(8,128)(2,1)} %param.13, bf16[16,512,1]{1,0,2:T(8,128)(2,1)S(1)} %fusion.19), kind=kOutput, calls=%fused_computation.36 | convolution fusion | flops 8388608 | bytes 8437760 | tf_op jit(solution)/shard_map/mij,mj->mi/dot_general | solution.py:324
  69.5 0.6 copy.18
  (8 shorter events, 0.1 us)
Async XLA Ops:
  21.1 2.4 %copy-start = (bf16[4,8,16,1152]{3,2,1,0:T(8,128)(2,1)S(1)}, bf16[4,8,16,1152]{3,2,1,0:T(8,128)(2,1)}, u32[]{:S(2)}) copy-start(bf16[4,8,16,1152]{3,2,1,0:T(8,128)(2,1)} %gather.2) | copy-start | bytes 3538948
  23.5 1.3 %copy-start.1 = (bf16[32,32,512]{2,1,0:T(8,128)(2,1)S(1)}, bf16[32,32,512]{2,1,0:T(8,128)(2,1)}, u32[]{:S(2)}) copy-start(bf16[32,32,512]{2,1,0:T(8,128)(2,1)} %param.7) | copy-start | bytes 3145732
  23.6 1.5 %copy-start.2 = (bf16[32,32,512]{2,1,0:T(8,128)(2,1)S(1)}, bf16[32,32,512]{2,1,0:T(8,128)(2,1)}, u32[]{:S(2)}) copy-start(bf16[32,32,512]{2,1,0:T(8,128)(2,1)} %param.8) | copy-start | bytes 3145732
  26.2 18.4 %copy-start.3 = (s32[16]{0:T(128)S(1)}, s32[16]{0:T(128)}, u32[]{:S(2)}) copy-start(s32[16]{0:T(128)} %param.12) | copy-start | bytes 196
  26.2 18.4 %copy-start.4 = (s32[16]{0:T(128)S(1)}, s32[16]{0:T(128)}, u32[]{:S(2)}) copy-start(s32[16]{0:T(128)} %param.11) | copy-start | bytes 196

commit v2 on v0

v2 whole, which is shorter than its diff:
```python
import math

import jax
import jax.numpy as jnp
from jax import lax
from jax.experimental import pallas as pl
from jax.experimental.pallas import tpu as pltpu
from jax.sharding import PartitionSpec as P

KL = 32
LANES = 128
MESH = pl.DeviceIdType.MESH


NT = (((1,), (1,)), ((), ()))


def mode_weight(index_x, index_z):
    return jnp.where(index_x > 0, 2.0, 1.0).astype(jnp.float32) * jnp.where(
        index_z > 0, 2.0, 1.0
    ).astype(jnp.float32)


def wrapped(phase, length):
    return phase & (length - 1) if length & (length - 1) == 0 else lax.rem(phase, length)


def copy_to(src, dst, send, recv, device):
    return pltpu.make_async_remote_copy(
        src_ref=src, dst_ref=dst, send_sem=send, recv_sem=recv, device_id=device, device_id_type=MESH
    )


class Place:
    def __init__(self, groups_x, groups_z):
        self.nx, self.nc = groups_x, groups_z // 2
        self.g = lax.axis_index("gx")
        gz = lax.axis_index("gz")
        self.gz = gz
        self.c, self.k = gz // 2, gz % 2

    def partner(self):
        return (self.g, 2 * self.c + 1 - self.k)

    def along_x(self, i):
        return lax.rem(self.g + i, self.nx)

    def along_c(self, j):
        return lax.rem(self.c + j, self.nc)


def greet(p):
    barrier = pltpu.get_barrier_semaphore()
    pl.semaphore_signal(barrier, inc=1, device_id=p.partner(), device_id_type=MESH)

    @pl.loop(1, p.nx)
    def _(i):
        pl.semaphore_signal(barrier, inc=1, device_id=(p.along_x(i), p.gz), device_id_type=MESH)

    @pl.loop(1, p.nc)
    def _(j):
        pl.semaphore_signal(
            barrier, inc=1, device_id=(p.g, 2 * p.along_c(j) + p.k), device_id_type=MESH
        )

    pl.semaphore_wait(barrier, 1 + p.nx - 1 + p.nc - 1)


class Gather:
    def __init__(self, p, out, send_x, send_c, send_p, recv):
        self.p, self.out = p, out
        self.send_x, self.send_c, self.send_p, self.recv = send_x, send_c, send_p, recv

    def at(self, g, gz):
        return self.out.at[g, gz]

    def to_x(self, i, c):
        p, gz = self.p, 2 * c + self.p.k
        return copy_to(
            self.at(p.g, gz), self.at(p.g, gz), self.send_x.at[i, c], self.recv.at[p.g, gz],
            (p.along_x(i), p.gz),
        )

    def to_c(self, j):
        p = self.p
        return copy_to(
            self.at(p.g, p.gz), self.at(p.g, p.gz), self.send_c.at[j], self.recv.at[p.g, p.gz],
            (p.g, 2 * p.along_c(j) + p.k),
        )

    def to_p(self, g, c):
        gz = 2 * c + self.p.k
        return copy_to(
            self.at(g, gz), self.at(g, gz), self.send_p.at[g, c], self.recv.at[g, gz],
            self.p.partner(),
        )

    def arrived(self, g, gz):
        copy_to(
            self.at(g, gz), self.at(g, gz), self.send_c.at[0], self.recv.at[g, gz],
            self.p.partner(),
        ).wait_recv()

    def start(self):
        p = self.p

        @pl.loop(1, p.nc)
        def _(j):
            self.to_c(j).start()

        @pl.loop(1, p.nx)
        def _(i):
            self.to_x(i, p.c).start()

        self.to_p(p.g, p.c).start()

    def relay_c(self):
        p = self.p

        @pl.loop(1, p.nc)
        def _(j):
            c = p.along_c(j)
            self.arrived(p.g, 2 * c + p.k)

            @pl.loop(1, p.nx)
            def _(i):
                self.to_x(i, c).start()

            self.to_p(p.g, c).start()

    def relay_x(self):
        p = self.p

        @pl.loop(0, p.nc)
        def _(j):
            c = p.along_c(j)

            @pl.loop(1, p.nx)
            def _(i):
                g = p.along_x(i)
                self.arrived(g, 2 * c + p.k)
                self.to_p(g, c).start()

    def from_partner(self, g):
        p = self.p

        @pl.loop(0, p.nc)
        def _(j):
            self.arrived(g, 2 * p.along_c(j) + 1 - p.k)

    def drain(self):
        p = self.p

        @pl.loop(1, p.nc)
        def _(j):
            self.to_c(j).wait_send()

        @pl.loop(0, p.nc)
        def _(c):
            @pl.loop(1, p.nx)
            def _(i):
                self.to_x(i, c).wait_send()

            @pl.loop(0, p.nx)
            def _(g):
                self.to_p(g, c).wait_send()


class Scatter:
    def __init__(self, p, part, pair, sums, from_x, acc, sent_c, from_c, sems):
        self.p, self.part, self.pair, self.sums, self.from_x = p, part, pair, sums, from_x
        self.acc, self.sent_c, self.from_c = acc, sent_c, from_c
        self.send_p, self.recv_p, self.send_x, self.recv_x, self.send_c, self.recv_c = sems

    def to_p(self, g):
        return copy_to(
            self.part.at[g, :, 1 - self.p.k], self.pair.at[g], self.send_p.at[g],
            self.recv_p.at[g], self.p.partner(),
        )

    def to_x(self, i):
        p = self.p
        g = p.along_x(i)
        return copy_to(
            self.sums.at[g], self.from_x.at[p.g], self.send_x.at[g], self.recv_x.at[p.g], (g, p.gz)
        )

    def to_c(self, j):
        p = self.p
        c = p.along_c(j)
        return copy_to(
            self.sent_c.at[c], self.from_c.at[p.c], self.send_c.at[c], self.recv_c.at[p.c],
            (p.g, 2 * c + p.k),
        )

    def chip_sum(self, g):
        self.to_p(g).wait_recv()
        return self.part[g, :, self.p.k] + self.pair[g]

    def across_x(self):
        p = self.p

        @pl.loop(1, p.nx)
        def _(i):
            g = p.along_x(i)
            self.sums[g] = self.chip_sum(g).astype(self.sums.dtype)
            self.to_x(i).start()

        self.acc[...] = self.chip_sum(p.g)

    def across_c(self):
        p = self.p

        @pl.loop(1, p.nx)
        def _(i):
            g = p.along_x(i)
            copy_to(
                self.sums.at[g], self.from_x.at[g], self.send_x.at[g], self.recv_x.at[g], p.partner()
            ).wait_recv()
            self.acc[...] += self.from_x[g].astype(jnp.float32)

        @pl.loop(1, p.nc)
        def _(j):
            c = p.along_c(j)
            self.sent_c[c] = self.acc[c].astype(self.sent_c.dtype)
            self.to_c(j).start()

    def total(self):
        p = self.p

        @pl.loop(1, p.nc)
        def _(j):
            c = p.along_c(j)
            copy_to(
                self.sent_c.at[c], self.from_c.at[c], self.send_c.at[c], self.recv_c.at[c],
                p.partner(),
            ).wait_recv()
            self.acc[p.c] += self.from_c[c].astype(jnp.float32)

        return self.acc[p.c]

    def drain(self):
        p = self.p

        @pl.loop(0, p.nx)
        def _(g):
            self.to_p(g).wait_send()

        @pl.loop(1, p.nx)
        def _(i):
            self.to_x(i).wait_send()

        @pl.loop(1, p.nc)
        def _(j):
            self.to_c(j).wait_send()


SCATTER_SEMS = 6


def step_kernel(
    groups_x, groups_z,
    high_u, high_v, low_u, low_v, labels, weight, tau,
    high_term, response,
    fine_u, fine_v, inverse, every, tables_t, tables, cross, products, mirror, answer, all_cross,
    load, first_sems, second_sems, cross_buffers, self_buffers,
):
    p = Place(groups_x, groups_z)
    cells_x, cells_z, levels = fine_u.shape
    points = cells_x * cells_z
    rows = low_u.shape[0]
    group = groups_z * rows
    lengths = (groups_x * cells_x, groups_z * cells_z)
    unitary = 1.0 / math.sqrt(lengths[0] * lengths[1])

    mine = every.at[p.g, p.gz]
    own = [
        pltpu.make_async_copy(low_u, mine.at[:, pl.ds(0, levels)], load.at[0]),
        pltpu.make_async_copy(low_v, mine.at[:, pl.ds(levels, levels)], load.at[1]),
        pltpu.make_async_copy(labels, mine.at[:, pl.ds(2 * levels, LANES)], load.at[2]),
    ]
    fields = [
        pltpu.make_async_copy(high_u, fine_u, load.at[3]),
        pltpu.make_async_copy(high_v, fine_v, load.at[4]),
        pltpu.make_async_copy(tau, inverse, load.at[5]),
    ]
    for copy in own + fields:
        copy.start()
    greet(p)
    for copy in own:
        copy.wait()
    first = Gather(p, every, *first_sems)
    first.start()

    lane = lax.broadcasted_iota(jnp.int32, (group, LANES), 1)
    on_x = lane < cells_x
    place = jnp.where(on_x, p.g * cells_x + lane, p.gz * cells_z + lane - cells_x)
    first.relay_c()
    first.relay_x()

    def build(i, _):
        g = p.along_x(i)
        first.from_partner(g)
        index = every[g, :, :, pl.ds(2 * levels, LANES)].reshape(group, LANES)
        index = index.astype(jnp.float32).astype(jnp.int32)
        even = index <= KL
        phase = jnp.where(even, index, index - KL) * place

        def angle(length):
            shifted = jnp.where(even, phase, phase + (length - length // 4))
            return wrapped(shifted, length).astype(jnp.float32) * (2.0 * math.pi / length)

        table = jnp.cos(jnp.where(on_x, angle(lengths[0]), angle(lengths[1])))
        turned = table.T
        along_z = turned[cells_x : cells_x + cells_z, :]
        at = pl.ds(pl.multiple_of(g * group, LANES), group)
        for x in range(cells_x):
            slab = turned[x : x + 1, :] * along_z
            tables_t[pl.ds(x * cells_z, cells_z), at] = slab.astype(tables_t.dtype)
        return 0

    lax.fori_loop(0, p.nx, build, 0)

    def turn(g, _):
        at = pl.ds(pl.multiple_of(g * group, LANES), group)
        tables[at, :] = tables_t[:, at].T
        return 0

    lax.fori_loop(0, p.nx, turn, 0)

    fields[0].wait()
    fields[1].wait()
    modes = groups_x * group
    block = 256 if points % 256 == 0 else points
    planes = block // cells_z

    def multiply(b, _):
        at = pl.ds(pl.multiple_of(b * block, block), block)
        held = every[:, :, :, pl.ds(0, 2 * levels)].reshape(modes, 2 * levels)
        coarse = jnp.dot(tables_t[at, :], held, preferred_element_type=jnp.float32)
        coarse_u, coarse_v = coarse[:, :levels], coarse[:, levels:]
        u = fine_u[pl.ds(b * planes, planes)].reshape(block, levels).astype(jnp.float32)
        v = fine_v[pl.ds(b * planes, planes)].reshape(block, levels).astype(jnp.float32)
        mixed = coarse_u * v + u * coarse_v
        cross[at, :] = mixed
        products[0, at, :] = mixed.astype(products.dtype)
        products[1, at, :] = (coarse_u * coarse_v + u * v).astype(products.dtype)
        return 0

    lax.fori_loop(0, points // block, multiply, 0)

    def project(scatter, which):
        def one(i, _):
            g = p.along_x(i)
            at = pl.ds(pl.multiple_of(g * group, LANES), group)
            scatter.part[g] = jnp.dot(
                tables[at, :], products[which], preferred_element_type=jnp.float32
            ).reshape(p.nc, 2, rows, levels)
            scatter.to_p(g).start()
            return 0

        lax.fori_loop(1, p.nx + 1, one, 0)

    crossed = Scatter(p, *cross_buffers)
    selfed = Scatter(p, *self_buffers)
    project(crossed, 0)
    crossed.across_x()
    project(selfed, 1)
    selfed.across_x()
    crossed.across_c()
    selfed.across_c()
    all_cross[p.g, p.gz] = (weight[:, 0:1] * (crossed.total() * unitary)).astype(all_cross.dtype)
    second = Gather(p, all_cross, *second_sems)
    second.start()
    forcing = (selfed.total() * unitary).astype(jnp.bfloat16)
    fields[2].wait()
    row = lax.broadcasted_iota(jnp.int32, (rows, levels), 0)
    answer[...] = jnp.zeros_like(answer)

    def solve(m, _):
        full = lax.dot_general(forcing, inverse[m], NT, preferred_element_type=jnp.float32)
        answer[...] += jnp.where(row == m, full, 0.0)
        return 0

    lax.fori_loop(0, rows // 2, solve, 0)
    second.relay_c()
    lax.fori_loop(rows // 2, rows, solve, 0)
    second.relay_x()
    response[...] = answer[...]

    @pl.loop(0, p.nx)
    def _(g):
        second.from_partner(g)

    def finish(b, _):
        at = pl.ds(pl.multiple_of(b * block, block), block)
        held = all_cross[...].reshape(modes, levels)
        restored = jnp.dot(tables_t[at, :], held, preferred_element_type=jnp.float32)
        part = (cross[at, :] - unitary * restored).astype(mirror.dtype)
        mirror[pl.ds(b * planes, planes)] = part.reshape(planes, cells_z, levels)
        writing(b).start()
        return 0

    def writing(b):
        at = pl.ds(b * planes, planes)
        return pltpu.make_async_copy(mirror.at[at], high_term.at[at], load.at[6 + b])

    lax.fori_loop(0, points // block, finish, 0)
    first.drain()
    second.drain()
    crossed.drain()
    selfed.drain()

    @pl.loop(0, points // block)
    def _(b):
        writing(b).wait()


def on_device(high_u, high_v, low_u, low_v, low_kx, low_kz, tau_inverse):
    cells_x, cells_z, levels = high_u.shape
    groups_x, groups_z = lax.axis_size("gx"), lax.axis_size("gz")
    chips, rows = groups_z // 2, low_u.shape[0]
    points = cells_x * cells_z
    modes = groups_x * groups_z * rows
    lane = jnp.arange(LANES, dtype=jnp.int32)[None, :]
    labels = jnp.where(lane < cells_x, low_kx[:, None], low_kz[:, None]).astype(jnp.bfloat16)
    weight = jnp.broadcast_to(mode_weight(low_kx, low_kz)[:, None], (rows, LANES))
    dma = pltpu.SemaphoreType.DMA
    narrow, wide = jnp.bfloat16, jnp.float32
    gather_sems = [
        dma((groups_x, chips)), dma((chips,)), dma((groups_x, chips)), dma((groups_x, groups_z)),
    ]
    scatter_buffers = [
        pltpu.VMEM((groups_x, chips, 2, rows, levels), wide),
        pltpu.VMEM((groups_x, chips, rows, levels), wide),
        pltpu.VMEM((groups_x, chips, rows, levels), narrow),
        pltpu.VMEM((groups_x, chips, rows, levels), narrow),
        pltpu.VMEM((chips, rows, levels), wide),
        pltpu.VMEM((chips, rows, levels), narrow),
        pltpu.VMEM((chips, rows, levels), narrow),
        [dma((groups_x,))] * 4 + [dma((chips,))] * 2,
    ]
    vmem, anywhere = pl.BlockSpec(memory_space=pltpu.VMEM), pl.BlockSpec(memory_space=pl.ANY)

    def body(*refs):
        step_kernel(groups_x, groups_z, *refs)

    return pl.pallas_call(
        body,
        out_shape=(
            jax.ShapeDtypeStruct(high_u.shape, narrow),
            jax.ShapeDtypeStruct((rows, levels), wide),
        ),
        in_specs=[anywhere, anywhere, vmem, vmem, vmem, vmem, anywhere],
        out_specs=(anywhere, vmem),
        scratch_shapes=[
            pltpu.VMEM(high_u.shape, narrow),
            pltpu.VMEM(high_u.shape, narrow),
            pltpu.VMEM(tau_inverse.shape, narrow),
            pltpu.VMEM((groups_x, groups_z, rows, 2 * levels + LANES), narrow),
            pltpu.VMEM((points, modes), narrow),
            pltpu.VMEM((modes, points), narrow),
            pltpu.VMEM((points, levels), wide),
            pltpu.VMEM((2, points, levels), narrow),
            pltpu.VMEM(high_u.shape, narrow),
            pltpu.VMEM((rows, levels), wide),
            pltpu.VMEM((groups_x, groups_z, rows, levels), narrow),
            dma((7 + points // 256,)),
            gather_sems,
            gather_sems,
            scatter_buffers,
            scatter_buffers,
        ],
        compiler_params=pltpu.CompilerParams(
            collective_id=0, has_side_effects=True, vmem_limit_bytes=60 * 1024 * 1024
        ),
        name="step",
    )(high_u, high_v, low_u, low_v, labels, weight, tau_inverse)


def solution(mesh):
    placed = (
        P("gx", "gz", None),
        P("gx", "gz", None),
        P(("gx", "gz"), None),
        P(("gx", "gz"), None),
        P(("gx", "gz")),
        P(("gx", "gz")),
        P(("gx", "gz"), None, None),
    )
    return jax.shard_map(
        on_device,
        mesh=mesh,
        in_specs=placed,
        out_specs=(P("gx", "gz", None), P(("gx", "gz"), None)),
        check_vma=False,
    )
```

time: 266 us -> 52.9 us (0.20)
  blocking collectives: 167 us -> 0 us
  waiting for transfers between devices: 58.8 us -> 0 us
  Pallas kernels: 0 us -> 45.6 us
  between operations: 14.2 us -> 0.64 us
  matrix products: 11.2 us -> 0 us
  local copies, waits for them, and re-layouts: 9.08 us -> 4.35 us
  other arithmetic: 5.06 us -> 2.02 us
    all_gather x3 -> x0, blocking collectives: 126 us -> none  [the longest x1 43.7 us: on_device(): lax.all_gather(cross_low, ('gx', 'gz'), axis=0, tiled=True)]
    reduce_scatter x2 -> x0, waiting for transfers between devices: 58.8 us -> none  [the longest x1 31.1 us: on_device(): lax.psum_scatter(jnp.dot(table, products, preferred_element_type=jnp.floa...]
    pallas_call x0 -> x1, Pallas kernels: none -> 45.6 us  [on_device(): pl.pallas_call(body, out_shape=(jax.ShapeDtypeStruct(high_u.shape, narrow...]
    unnamed x1 -> x0, blocking collectives: 40.5 us -> none
    dot_general x4 -> x0, matrix products: 11.2 us -> none  [the longest x1 5.63 us: on_device(): jnp.einsum('mij,mj->mi', tau_inverse, forcing.astype(jnp.bfloat16), prefe...]
    gather x2 -> x0, local copies, waits for them, and re-layouts: 6.98 us -> none  [on_device(): table = patterns(jnp.take(every_x, modes), jnp.take(every_z, modes))]
    unnamed x16 -> x2, local copies, waits for them, and re-layouts: 0.7 us -> 3.68 us
  transfers between devices with their start and end apart: 2 -> 0, of which waited for: 2 -> 0; matrix products, arithmetic and copies ran while one was open for 0% -> 0% of each run, Pallas kernels for 0% -> 0%
where the time goes in v2:
time: 52.9 us; the launch traced here: 52.6 us
  Pallas kernels  45.6 us (86%)
  local copies, waits for them, and re-layouts  4.35 us (8%)
  other arithmetic  2.02 us (4%)
  between operations  0.64 us (1%)
    pallas_call x1, Pallas kernels, on_device(): pl.pallas_call(body, out_shape=(jax.ShapeDtypeStruct(high_u.shape, narrow...  45.6 us
    unnamed x2, local copies, waits for them, and re-layouts  3.68 us
    convert_element_type x1, other arithmetic, on_device(): jnp.where(lane < cells_x, low_kx[:, None], low_kz[:, None])  1.34 us

profile of v2, /device:TPU:1, one launch (start us, length us, event | category | flops | bytes accessed | tf_op | source)
XLA Modules:
  0.0 52.6 jit_solution(14481213326307450030)
XLA Ops:
  0.6 0.7 %fusion = f32[16]{0:T(128)S(1)} fusion(s32[16]{0:T(128)} %param.11, s32[16]{0:T(128)} %param.12), kind=kLoop, calls=%fused_computation.3 | loop fusion | flops 80 | bytes 192 | tf_op jit(solution)/shard_map/mul | solution.py:19
  1.3 1.3 %select_convert_fusion.refs_4_ = bf16[16,128]{1,0:T(8,128)(2,1)} fusion(s32[16]{0:T(128)} %param.12, s32[16]{0:T(128)} %param.11, pred[128]{0:T(512)(128)(4,1)S(1)} %iota_compare_fusion), kind=kLoop, calls=%fused_computation | loop fusion | flops 4096 | bytes 4352 | tf_op jit(solution)/shard_map/convert_element_type | solution.py:426
  2.6 0.7 %broadcast_in_dim.48.refs_5_ = f32[16,128]{1,0:T(8,128)} broadcast(f32[16]{0:T(128)S(1)} %fusion), dimensions={0} | broadcast | bytes 8256 | tf_op jit(solution)/shard_map/broadcast_in_dim | solution.py:427
  3.3 45.6 %step.1 = (bf16[32,32,512]{2,1,0:T(8,128)(2,1)}, f32[16,512]{1,0:T(8,128)}) custom-call(bf16[32,32,512]{2,1,0:T(8,128)(2,1)} %refs_0_.1, bf16[32,32,512]{2,1,0:T(8,128)(2,1)} %refs_1_.1, bf16[16,512]{1,0:T(8,128)(2,1)} %refs_2_.1, bf16[16,512]{1,0:T(8,128)(2,1)} %refs_3_.1, bf16[16,128]{1,0:T(8,128)(2,1)} %select_convert_fusion.refs_4_, ...), custom_call_target="tpu_custom_call" | custom-call | tf_op jit(solution)/shard_map/step/pallas_call | solution.py:448
  48.9 2.3 %copy.11 = bf16[32,32,512]{2,1,0:T(8,128)(2,1)} copy(bf16[32,32,512]{2,1,0:T(8,128)(2,1)} %get-tuple-element.4) | data formatting | bytes 2097152
  51.2 1.4 %copy.12 = f32[16,512]{1,0:T(8,128)} copy(f32[16,512]{1,0:T(8,128)} %get-tuple-element.5) | data formatting | bytes 65536
  (1 shorter events, 0.0 us)

commit v3 on v2

--- a/solution.py
+++ b/solution.py
@@ -15,14 +15,12 @@
 NT = (((1,), (1,)), ((), ()))
 
 
-def mode_weight(index_x, index_z):
-    return jnp.where(index_x > 0, 2.0, 1.0).astype(jnp.float32) * jnp.where(
-        index_z > 0, 2.0, 1.0
-    ).astype(jnp.float32)
-
-
 def wrapped(phase, length):
     return phase & (length - 1) if length & (length - 1) == 0 else lax.rem(phase, length)
+
+
+def row_block(points):
+    return 256 if points % 256 == 0 else points
 
 
 def copy_to(src, dst, send, recv, device):
@@ -255,14 +253,15 @@
             self.to_c(j).wait_send()
 
 
-SCATTER_SEMS = 6
+LIMIT_ONE = 48 * 1024 * 1024
+LIMIT_TWO = 16 * 1024 * 1024
 
 
 def step_kernel(
     groups_x, groups_z,
-    high_u, high_v, low_u, low_v, labels, weight, tau,
-    high_term, response,
-    fine_u, fine_v, inverse, every, tables_t, tables, cross, products, mirror, answer, all_cross,
+    high_u, high_v, low_u, low_v, low_kx, low_kz, tau,
+    cross, tables_t, all_cross, answer,
+    fine_u, fine_v, inverse, every, tables, products,
     load, first_sems, second_sems, cross_buffers, self_buffers,
 ):
     p = Place(groups_x, groups_z)
@@ -277,7 +276,6 @@
     own = [
         pltpu.make_async_copy(low_u, mine.at[:, pl.ds(0, levels)], load.at[0]),
         pltpu.make_async_copy(low_v, mine.at[:, pl.ds(levels, levels)], load.at[1]),
-        pltpu.make_async_copy(labels, mine.at[:, pl.ds(2 * levels, LANES)], load.at[2]),
     ]
     fields = [
         pltpu.make_async_copy(high_u, fine_u, load.at[3]),
@@ -286,6 +284,17 @@
     ]
     for copy in own + fields:
         copy.start()
+    slot = lax.broadcasted_iota(jnp.int32, (rows, rows), 0)
+    straight = slot == lax.broadcasted_iota(jnp.int32, (rows, rows), 1)
+
+    def upright(line):
+        spread = jnp.broadcast_to(line[...].astype(jnp.float32), (rows, rows))
+        return jnp.sum(jnp.where(straight, spread, 0.0), axis=1, keepdims=True)
+
+    kx, kz = upright(low_kx), upright(low_kz)
+    weight = jnp.where(kx > 0, 2.0, 1.0) * jnp.where(kz > 0, 2.0, 1.0)
+    first_lanes = lax.broadcasted_iota(jnp.int32, (rows, LANES), 1) < cells_x
+    every[p.g, p.gz, :, pl.ds(2 * levels, LANES)] = jnp.where(first_lanes, kx, kz).astype(every.dtype)
     greet(p)
     for copy in own:
         copy.wait()
@@ -331,7 +340,7 @@
     fields[0].wait()
     fields[1].wait()
     modes = groups_x * group
-    block = 256 if points % 256 == 0 else points
+    block = row_block(points)
     planes = block // cells_z
 
     def multiply(b, _):
@@ -369,7 +378,7 @@
     selfed.across_x()
     crossed.across_c()
     selfed.across_c()
-    all_cross[p.g, p.gz] = (weight[:, 0:1] * (crossed.total() * unitary)).astype(all_cross.dtype)
+    all_cross[p.g, p.gz] = (weight * (crossed.total() * unitary)).astype(all_cross.dtype)
     second = Gather(p, all_cross, *second_sems)
     second.start()
     forcing = (selfed.total() * unitary).astype(jnp.bfloat16)
@@ -386,11 +395,28 @@
     second.relay_c()
     lax.fori_loop(rows // 2, rows, solve, 0)
     second.relay_x()
-    response[...] = answer[...]
 
     @pl.loop(0, p.nx)
     def _(g):
         second.from_partner(g)
+
+    first.drain()
+    second.drain()
+    crossed.drain()
+    selfed.drain()
+
+
+def finish_kernel(unitary, cross, tables_t, all_cross, answer, high_term, response, mirror, sems):
+    points, levels = cross.shape
+    cells_z = high_term.shape[1]
+    block = row_block(points)
+    planes = block // cells_z
+    modes = tables_t.shape[1]
+    response[...] = answer[...]
+
+    def writing(b):
+        at = pl.ds(b * planes, planes)
+        return pltpu.make_async_copy(mirror.at[at], high_term.at[at], sems.at[b])
 
     def finish(b, _):
         at = pl.ds(pl.multiple_of(b * block, block), block)
@@ -401,15 +427,7 @@
         writing(b).start()
         return 0
 
-    def writing(b):
-        at = pl.ds(b * planes, planes)
-        return pltpu.make_async_copy(mirror.at[at], high_term.at[at], load.at[6 + b])
-
     lax.fori_loop(0, points // block, finish, 0)
-    first.drain()
-    second.drain()
-    crossed.drain()
-    selfed.drain()
 
     @pl.loop(0, points // block)
     def _(b):
@@ -422,9 +440,6 @@
     chips, rows = groups_z // 2, low_u.shape[0]
     points = cells_x * cells_z
     modes = groups_x * groups_z * rows
-    lane = jnp.arange(LANES, dtype=jnp.int32)[None, :]
-    labels = jnp.where(lane < cells_x, low_kx[:, None], low_kz[:, None]).astype(jnp.bfloat16)
-    weight = jnp.broadcast_to(mode_weight(low_kx, low_kz)[:, None], (rows, LANES))
     dma = pltpu.SemaphoreType.DMA
     narrow, wide = jnp.bfloat16, jnp.float32
     gather_sems = [
@@ -440,42 +455,56 @@
         pltpu.VMEM((chips, rows, levels), narrow),
         [dma((groups_x,))] * 4 + [dma((chips,))] * 2,
     ]
-    vmem, anywhere = pl.BlockSpec(memory_space=pltpu.VMEM), pl.BlockSpec(memory_space=pl.ANY)
+    vmem, hbm = pl.BlockSpec(memory_space=pltpu.VMEM), pl.BlockSpec(memory_space=pltpu.HBM)
 
     def body(*refs):
         step_kernel(groups_x, groups_z, *refs)
 
-    return pl.pallas_call(
+    cross, tables_t, all_cross, answer = pl.pallas_call(
         body,
         out_shape=(
-            jax.ShapeDtypeStruct(high_u.shape, narrow),
+            jax.ShapeDtypeStruct((points, levels), wide),
+            jax.ShapeDtypeStruct((points, modes), narrow),
+            jax.ShapeDtypeStruct((groups_x, groups_z, rows, levels), narrow),
             jax.ShapeDtypeStruct((rows, levels), wide),
         ),
-        in_specs=[anywhere, anywhere, vmem, vmem, vmem, vmem, anywhere],
-        out_specs=(anywhere, vmem),
+        in_specs=[hbm, hbm, hbm, hbm, vmem, vmem, hbm],
+        out_specs=(vmem, vmem, vmem, vmem),
         scratch_shapes=[
             pltpu.VMEM(high_u.shape, narrow),
             pltpu.VMEM(high_u.shape, narrow),
             pltpu.VMEM(tau_inverse.shape, narrow),
             pltpu.VMEM((groups_x, groups_z, rows, 2 * levels + LANES), narrow),
-            pltpu.VMEM((points, modes), narrow),
             pltpu.VMEM((modes, points), narrow),
-            pltpu.VMEM((points, levels), wide),
             pltpu.VMEM((2, points, levels), narrow),
-            pltpu.VMEM(high_u.shape, narrow),
-            pltpu.VMEM((rows, levels), wide),
-            pltpu.VMEM((groups_x, groups_z, rows, levels), narrow),
-            dma((7 + points // 256,)),
+            dma((6,)),
             gather_sems,
             gather_sems,
             scatter_buffers,
             scatter_buffers,
         ],
         compiler_params=pltpu.CompilerParams(
-            collective_id=0, has_side_effects=True, vmem_limit_bytes=60 * 1024 * 1024
+            collective_id=0, has_side_effects=True, vmem_limit_bytes=LIMIT_ONE
         ),
         name="step",
-    )(high_u, high_v, low_u, low_v, labels, weight, tau_inverse)
+    )(high_u, high_v, low_u, low_v, low_kx.reshape(1, rows), low_kz.reshape(1, rows), tau_inverse)
+    unitary = 1.0 / math.sqrt(groups_x * cells_x * groups_z * cells_z)
+
+    def last(*refs):
+        finish_kernel(unitary, *refs)
+
+    return pl.pallas_call(
+        last,
+        out_shape=(
+            jax.ShapeDtypeStruct(high_u.shape, narrow),
+            jax.ShapeDtypeStruct((rows, levels), wide),
+        ),
+        in_specs=[vmem, vmem, vmem, vmem],
+        out_specs=(hbm, vmem),
+        scratch_shapes=[pltpu.VMEM(high_u.shape, narrow), dma((points // row_block(points),))],
+        compiler_params=pltpu.CompilerParams(vmem_limit_bytes=LIMIT_TWO),
+        name="finish",
+    )(cross, tables_t, all_cross, answer)
 
 
 def solution(mesh):

time: 52.9 us -> 51.8 us (0.979)
  other arithmetic: 2.02 us -> 0 us
  local copies, waits for them, and re-layouts: 4.35 us -> 5.19 us
    unnamed x2 -> x12, local copies, waits for them, and re-layouts: 3.68 us -> 5.19 us
    convert_element_type x1 -> x0, other arithmetic: 1.34 us -> none  [on_device(): jnp.where(lane < cells_x, low_kx[:, None], low_kz[:, None])]
    mul x1 -> x0, other arithmetic: 0.68 us -> none  [mode_weight(): jnp.where(index_x > 0, 2.0, 1.0).astype(jnp.float32)]
    broadcast_in_dim x1 -> x0, local copies, waits for them, and re-layouts: 0.67 us -> none  [on_device(): jnp.broadcast_to(mode_weight(low_kx, low_kz)[:, None], (rows, LANES))]
    pallas_call x1 -> x2, Pallas kernels: 45.6 us -> 45.6 us  [the longest x1 43 us: on_device(): pl.pallas_call(body, out_shape=(jax.ShapeDtypeStruct((points, levels), wi...]
where the time goes in v3:
time: 51.8 us; the launch traced here: 51.5 us
  Pallas kernels  45.6 us (88%)
  local copies, waits for them, and re-layouts  5.19 us (10%)
  between operations  0.65 us (1%)
    pallas_call x1, Pallas kernels, on_device(): pl.pallas_call(body, out_shape=(jax.ShapeDtypeStruct((points, levels), wi...  43 us
    unnamed x12, local copies, waits for them, and re-layouts  5.19 us
    pallas_call x1, Pallas kernels, on_device(): pl.pallas_call(last, out_shape=(jax.ShapeDtypeStruct(high_u.shape, narrow...  2.57 us

profile of v3, /device:TPU:1, one launch (start us, length us, event | category | flops | bytes accessed | tf_op | source)
XLA Modules:
  0.0 51.5 jit_solution(10981147960985032178)
XLA Ops:
  0.6 0.0 copy-start
  0.6 1.2 %copy-done = bf16[32,32,512]{2,1,0:T(8,128)(2,1)S(1)} copy-done((bf16[32,32,512]{2,1,0:T(8,128)(2,1)S(1)}, bf16[32,32,512]{2,1,0:T(8,128)(2,1)}, u32[]{:S(2)}) %copy-start) | copy-done | bytes 1048600
  1.9 0.0 copy-start.1
  1.9 1.2 %copy-done.1 = bf16[32,32,512]{2,1,0:T(8,128)(2,1)S(1)} copy-done((bf16[32,32,512]{2,1,0:T(8,128)(2,1)S(1)}, bf16[32,32,512]{2,1,0:T(8,128)(2,1)}, u32[]{:S(2)}) %copy-start.1) | copy-done | bytes 1048600
  3.1 0.0 copy-start.2
  3.1 0.7 %copy-done.2 = bf16[16,512]{1,0:T(8,128)(2,1)S(1)} copy-done((bf16[16,512]{1,0:T(8,128)(2,1)S(1)}, bf16[16,512]{1,0:T(8,128)(2,1)}, u32[]{:S(2)}) %copy-start.2) | copy-done | bytes 16408
  3.8 0.0 copy-start.3
  3.8 0.7 %copy-done.3 = bf16[16,512]{1,0:T(8,128)(2,1)S(1)} copy-done((bf16[16,512]{1,0:T(8,128)(2,1)S(1)}, bf16[16,512]{1,0:T(8,128)(2,1)}, u32[]{:S(2)}) %copy-start.3) | copy-done | bytes 16408
  4.5 0.0 copy-start.4
  4.5 0.7 %copy-done.4 = s32[16]{0:T(128)S(1)} copy-done((s32[16]{0:T(128)S(1)}, s32[16]{0:T(128)}, u32[]{:S(2)}) %copy-start.4) | copy-done | bytes 88
  5.2 0.0 copy-start.5
  5.2 0.7 %copy-done.5 = s32[16]{0:T(128)S(1)} copy-done((s32[16]{0:T(128)S(1)}, s32[16]{0:T(128)}, u32[]{:S(2)}) %copy-start.5) | copy-done | bytes 88
  5.8 43.0 %step.1 = (f32[1024,512]{1,0:T(8,128)S(1)}, bf16[1024,512]{1,0:T(8,128)(2,1)S(1)}, bf16[4,8,16,512]{3,2,1,0:T(8,128)(2,1)S(1)}, f32[16,512]{1,0:T(8,128)S(1)}) custom-call(bf16[32,32,512]{2,1,0:T(8,128)(2,1)S(1)} %copy-done, bf16[32,32,512]{2,1,0:T(8,128)(2,1)S(1)} %copy-done.1, bf16[16,512]{1,0:T(8,128)(2,1)S(1)} %copy-done.2, ...), custom_call_target="tpu_custom_call" | custom-call | tf_op jit(solution)/shard_map/step/pallas_call | solution.py:463
  48.9 2.6 %finish.1 = (bf16[32,32,512]{2,1,0:T(8,128)(2,1)}, f32[16,512]{1,0:T(8,128)}) custom-call(f32[1024,512]{1,0:T(8,128)S(1)} %get-tuple-element.6.refs_0_, bf16[1024,512]{1,0:T(8,128)(2,1)S(1)} %get-tuple-element.7.refs_1_, bf16[4,8,16,512]{3,2,1,0:T(8,128)(2,1)S(1)} %get-tuple-element.8.refs_2_, f32[16,512]{1,0:T(8,128)S(1)} %get-tuple-element.9.refs_3_), custom_call_target="tpu_custom_call" | custom-call | tf_op jit(solution)/shard_map/finish/pallas_call | solution.py:496
Async XLA Ops:
  0.6 1.2 %copy-start = (bf16[32,32,512]{2,1,0:T(8,128)(2,1)S(1)}, bf16[32,32,512]{2,1,0:T(8,128)(2,1)}, u32[]{:S(2)}) copy-start(bf16[32,32,512]{2,1,0:T(8,128)(2,1)} %refs_0_.1) | copy-start | bytes 3145732
  1.9 1.2 %copy-start.1 = (bf16[32,32,512]{2,1,0:T(8,128)(2,1)S(1)}, bf16[32,32,512]{2,1,0:T(8,128)(2,1)}, u32[]{:S(2)}) copy-start(bf16[32,32,512]{2,1,0:T(8,128)(2,1)} %refs_1_.1) | copy-start | bytes 3145732
  3.1 0.7 %copy-start.2 = (bf16[16,512]{1,0:T(8,128)(2,1)S(1)}, bf16[16,512]{1,0:T(8,128)(2,1)}, u32[]{:S(2)}) copy-start(bf16[16,512]{1,0:T(8,128)(2,1)} %refs_2_.1) | copy-start | bytes 49156
  3.8 0.7 %copy-start.3 = (bf16[16,512]{1,0:T(8,128)(2,1)S(1)}, bf16[16,512]{1,0:T(8,128)(2,1)}, u32[]{:S(2)}) copy-start(bf16[16,512]{1,0:T(8,128)(2,1)} %refs_3_.1) | copy-start | bytes 49156
  4.5 0.7 %copy-start.4 = (s32[16]{0:T(128)S(1)}, s32[16]{0:T(128)}, u32[]{:S(2)}) copy-start(s32[16]{0:T(128)} %param.11) | copy-start | bytes 196
  5.2 0.7 %copy-start.5 = (s32[16]{0:T(128)S(1)}, s32[16]{0:T(128)}, u32[]{:S(2)}) copy-start(s32[16]{0:T(128)} %param.12) | copy-start | bytes 196

commit v4 on v3

--- a/solution.py
+++ b/solution.py
@@ -261,7 +261,7 @@
     groups_x, groups_z,
     high_u, high_v, low_u, low_v, low_kx, low_kz, tau,
     cross, tables_t, all_cross, answer,
-    fine_u, fine_v, inverse, every, tables, products,
+    fine_u, fine_v, inverse, every, tables, products, lines,
     load, first_sems, second_sems, cross_buffers, self_buffers,
 ):
     p = Place(groups_x, groups_z)
@@ -282,16 +282,22 @@
         pltpu.make_async_copy(high_v, fine_v, load.at[4]),
         pltpu.make_async_copy(tau, inverse, load.at[5]),
     ]
-    for copy in own + fields:
+    indices = [
+        pltpu.make_async_copy(low_kx, lines.at[0], load.at[2]),
+        pltpu.make_async_copy(low_kz, lines.at[1], load.at[6]),
+    ]
+    for copy in indices + own + fields:
         copy.start()
     slot = lax.broadcasted_iota(jnp.int32, (rows, rows), 0)
     straight = slot == lax.broadcasted_iota(jnp.int32, (rows, rows), 1)
 
     def upright(line):
-        spread = jnp.broadcast_to(line[...].astype(jnp.float32), (rows, rows))
+        spread = jnp.broadcast_to(line.astype(jnp.float32), (rows, rows))
         return jnp.sum(jnp.where(straight, spread, 0.0), axis=1, keepdims=True)
 
-    kx, kz = upright(low_kx), upright(low_kz)
+    for copy in indices:
+        copy.wait()
+    kx, kz = upright(lines[0]), upright(lines[1])
     weight = jnp.where(kx > 0, 2.0, 1.0) * jnp.where(kz > 0, 2.0, 1.0)
     first_lanes = lax.broadcasted_iota(jnp.int32, (rows, LANES), 1) < cells_x
     every[p.g, p.gz, :, pl.ds(2 * levels, LANES)] = jnp.where(first_lanes, kx, kz).astype(every.dtype)
@@ -468,7 +474,7 @@
             jax.ShapeDtypeStruct((groups_x, groups_z, rows, levels), narrow),
             jax.ShapeDtypeStruct((rows, levels), wide),
         ),
-        in_specs=[hbm, hbm, hbm, hbm, vmem, vmem, hbm],
+        in_specs=[hbm] * 7,
         out_specs=(vmem, vmem, vmem, vmem),
         scratch_shapes=[
             pltpu.VMEM(high_u.shape, narrow),
@@ -477,7 +483,8 @@
             pltpu.VMEM((groups_x, groups_z, rows, 2 * levels + LANES), narrow),
             pltpu.VMEM((modes, points), narrow),
             pltpu.VMEM((2, points, levels), narrow),
-            dma((6,)),
+            pltpu.VMEM((2, 1, rows), jnp.int32),
+            dma((7,)),
             gather_sems,
             gather_sems,
             scatter_buffers,
@@ -487,7 +494,15 @@
             collective_id=0, has_side_effects=True, vmem_limit_bytes=LIMIT_ONE
         ),
         name="step",
-    )(high_u, high_v, low_u, low_v, low_kx.reshape(1, rows), low_kz.reshape(1, rows), tau_inverse)
+    )(
+        *(
+            pltpu.with_memory_space_constraint(array, pltpu.HBM)
+            for array in (
+                high_u, high_v, low_u, low_v, low_kx.reshape(1, rows), low_kz.reshape(1, rows),
+                tau_inverse,
+            )
+        )
+    )
     unitary = 1.0 / math.sqrt(groups_x * cells_x * groups_z * cells_z)
 
     def last(*refs):

time: 51.8 us -> 47 us (0.907)
  local copies, waits for them, and re-layouts: 5.19 us -> 0 us
  Pallas kernels: 45.6 us -> 46.2 us
    unnamed x12 -> x0, local copies, waits for them, and re-layouts: 5.19 us -> none
    pallas_call x1, Pallas kernels: 43 us -> 43.6 us  [on_device(): pl.pallas_call(body, out_shape=(jax.ShapeDtypeStruct((points, levels), wi...]
where the time goes in v4:
time: 47 us; the launch traced here: 46.8 us
  Pallas kernels  46.2 us (98%)
  between operations  0.64 us (1%)
    pallas_call x1, Pallas kernels, on_device(): pl.pallas_call(body, out_shape=(jax.ShapeDtypeStruct((points, levels), wi...  43.6 us
    pallas_call x1, Pallas kernels, on_device(): pl.pallas_call(last, out_shape=(jax.ShapeDtypeStruct(high_u.shape, narrow...  2.57 us

profile of v4, /device:TPU:1, one launch (start us, length us, event | category | flops | bytes accessed | tf_op | source)
XLA Modules:
  0.0 46.8 jit_solution(10938317665837522841)
XLA Ops:
  0.6 43.6 %step.1 = (f32[1024,512]{1,0:T(8,128)S(1)}, bf16[1024,512]{1,0:T(8,128)(2,1)S(1)}, bf16[4,8,16,512]{3,2,1,0:T(8,128)(2,1)S(1)}, f32[16,512]{1,0:T(8,128)S(1)}) custom-call(bf16[32,32,512]{2,1,0:T(8,128)(2,1)} %refs_0_.1, bf16[32,32,512]{2,1,0:T(8,128)(2,1)} %refs_1_.1, bf16[16,512]{1,0:T(8,128)(2,1)} %refs_2_.1, bf16[16,512]{1,0:T(8,128)(2,1)} %refs_3_.1, ...), custom_call_target="tpu_custom_call" | custom-call | tf_op jit(solution)/shard_map/step/pallas_call | solution.py:469
  44.2 2.6 %finish.1 = (bf16[32,32,512]{2,1,0:T(8,128)(2,1)}, f32[16,512]{1,0:T(8,128)}) custom-call(f32[1024,512]{1,0:T(8,128)S(1)} %get-tuple-element.6.refs_0_, bf16[1024,512]{1,0:T(8,128)(2,1)S(1)} %get-tuple-element.7.refs_1_, bf16[4,8,16,512]{3,2,1,0:T(8,128)(2,1)S(1)} %get-tuple-element.8.refs_2_, f32[16,512]{1,0:T(8,128)S(1)} %get-tuple-element.9.refs_3_), custom_call_target="tpu_custom_call" | custom-call | tf_op jit(solution)/shard_map/finish/pallas_call | solution.py:511

commit v5 on v4

--- a/solution.py
+++ b/solution.py
@@ -61,7 +61,7 @@
             barrier, inc=1, device_id=(p.g, 2 * p.along_c(j) + p.k), device_id_type=MESH
         )
 
-    pl.semaphore_wait(barrier, 1 + p.nx - 1 + p.nc - 1)
+    return lambda: pl.semaphore_wait(barrier, 1 + p.nx - 1 + p.nc - 1)
 
 
 class Gather:
@@ -261,10 +261,11 @@
     groups_x, groups_z,
     high_u, high_v, low_u, low_v, low_kx, low_kz, tau,
     cross, tables_t, all_cross, answer,
-    fine_u, fine_v, inverse, every, tables, products, lines,
-    load, first_sems, second_sems, cross_buffers, self_buffers,
+    fine_u, fine_v, inverse, every, tables, products, lines, marks,
+    load, ahead_sems, first_sems, second_sems, cross_buffers, self_buffers,
 ):
     p = Place(groups_x, groups_z)
+    all_here = greet(p)
     cells_x, cells_z, levels = fine_u.shape
     points = cells_x * cells_z
     rows = low_u.shape[0]
@@ -300,8 +301,10 @@
     kx, kz = upright(lines[0]), upright(lines[1])
     weight = jnp.where(kx > 0, 2.0, 1.0) * jnp.where(kz > 0, 2.0, 1.0)
     first_lanes = lax.broadcasted_iota(jnp.int32, (rows, LANES), 1) < cells_x
-    every[p.g, p.gz, :, pl.ds(2 * levels, LANES)] = jnp.where(first_lanes, kx, kz).astype(every.dtype)
-    greet(p)
+    marks[p.g, p.gz] = jnp.where(first_lanes, kx, kz).astype(marks.dtype)
+    all_here()
+    ahead = Gather(p, marks, *ahead_sems)
+    ahead.start()
     for copy in own:
         copy.wait()
     first = Gather(p, every, *first_sems)
@@ -310,13 +313,14 @@
     lane = lax.broadcasted_iota(jnp.int32, (group, LANES), 1)
     on_x = lane < cells_x
     place = jnp.where(on_x, p.g * cells_x + lane, p.gz * cells_z + lane - cells_x)
+    ahead.relay_c()
     first.relay_c()
-    first.relay_x()
+    ahead.relay_x()
 
     def build(i, _):
         g = p.along_x(i)
-        first.from_partner(g)
-        index = every[g, :, :, pl.ds(2 * levels, LANES)].reshape(group, LANES)
+        ahead.from_partner(g)
+        index = marks[g].reshape(group, LANES)
         index = index.astype(jnp.float32).astype(jnp.int32)
         even = index <= KL
         phase = jnp.where(even, index, index - KL) * place
@@ -342,6 +346,11 @@
         return 0
 
     lax.fori_loop(0, p.nx, turn, 0)
+    first.relay_x()
+
+    @pl.loop(0, p.nx)
+    def _(g):
+        first.from_partner(g)
 
     fields[0].wait()
     fields[1].wait()
@@ -351,7 +360,7 @@
 
     def multiply(b, _):
         at = pl.ds(pl.multiple_of(b * block, block), block)
-        held = every[:, :, :, pl.ds(0, 2 * levels)].reshape(modes, 2 * levels)
+        held = every[...].reshape(modes, 2 * levels)
         coarse = jnp.dot(tables_t[at, :], held, preferred_element_type=jnp.float32)
         coarse_u, coarse_v = coarse[:, :levels], coarse[:, levels:]
         u = fine_u[pl.ds(b * planes, planes)].reshape(block, levels).astype(jnp.float32)
@@ -406,6 +415,7 @@
     def _(g):
         second.from_partner(g)
 
+    ahead.drain()
     first.drain()
     second.drain()
     crossed.drain()
@@ -480,11 +490,13 @@
             pltpu.VMEM(high_u.shape, narrow),
             pltpu.VMEM(high_u.shape, narrow),
             pltpu.VMEM(tau_inverse.shape, narrow),
-            pltpu.VMEM((groups_x, groups_z, rows, 2 * levels + LANES), narrow),
+            pltpu.VMEM((groups_x, groups_z, rows, 2 * levels), narrow),
             pltpu.VMEM((modes, points), narrow),
             pltpu.VMEM((2, points, levels), narrow),
             pltpu.VMEM((2, 1, rows), jnp.int32),
+            pltpu.VMEM((groups_x, groups_z, rows, LANES), narrow),
             dma((7,)),
+            gather_sems,
             gather_sems,
             gather_sems,
             scatter_buffers,

time: 47 us -> 45.9 us (0.977)
  Pallas kernels: 46.2 us -> 45.1 us
    pallas_call x1, Pallas kernels: 43.6 us -> 42.5 us  [on_device(): pl.pallas_call(body, out_shape=(jax.ShapeDtypeStruct((points, levels), wi...]
where the time goes in v5:
time: 45.9 us; the launch traced here: 45.7 us
  Pallas kernels  45.1 us (98%)
  between operations  0.64 us (1%)
    pallas_call x1, Pallas kernels, on_device(): pl.pallas_call(body, out_shape=(jax.ShapeDtypeStruct((points, levels), wi...  42.5 us
    pallas_call x1, Pallas kernels, on_device(): pl.pallas_call(last, out_shape=(jax.ShapeDtypeStruct(high_u.shape, narrow...  2.57 us

profile of v5, /device:TPU:1, one launch (start us, length us, event | category | flops | bytes accessed | tf_op | source)
XLA Modules:
  0.0 45.7 jit_solution(8318895236009002553)
XLA Ops:
  0.6 42.5 %step.1 = (f32[1024,512]{1,0:T(8,128)S(1)}, bf16[1024,512]{1,0:T(8,128)(2,1)S(1)}, bf16[4,8,16,512]{3,2,1,0:T(8,128)(2,1)S(1)}, f32[16,512]{1,0:T(8,128)S(1)}) custom-call(bf16[32,32,512]{2,1,0:T(8,128)(2,1)} %refs_0_.1, bf16[32,32,512]{2,1,0:T(8,128)(2,1)} %refs_1_.1, bf16[16,512]{1,0:T(8,128)(2,1)} %refs_2_.1, bf16[16,512]{1,0:T(8,128)(2,1)} %refs_3_.1, ...), custom_call_target="tpu_custom_call" | custom-call | tf_op jit(solution)/shard_map/step/pallas_call | solution.py:479
  43.1 2.6 %finish.1 = (bf16[32,32,512]{2,1,0:T(8,128)(2,1)}, f32[16,512]{1,0:T(8,128)}) custom-call(f32[1024,512]{1,0:T(8,128)S(1)} %get-tuple-element.6.refs_0_, bf16[1024,512]{1,0:T(8,128)(2,1)S(1)} %get-tuple-element.7.refs_1_, bf16[4,8,16,512]{3,2,1,0:T(8,128)(2,1)S(1)} %get-tuple-element.8.refs_2_, f32[16,512]{1,0:T(8,128)S(1)} %get-tuple-element.9.refs_3_), custom_call_target="tpu_custom_call" | custom-call | tf_op jit(solution)/shard_map/finish/pallas_call | solution.py:523

commit v6 on v5

--- a/solution.py
+++ b/solution.py
@@ -165,14 +165,15 @@
 
 
 class Scatter:
-    def __init__(self, p, part, pair, sums, from_x, acc, sent_c, from_c, sems):
-        self.p, self.part, self.pair, self.sums, self.from_x = p, part, pair, sums, from_x
+    def __init__(self, p, part, thin, pair, sums, from_x, acc, sent_c, from_c, sems):
+        self.p, self.part, self.thin, self.pair = p, part, thin, pair
+        self.sums, self.from_x = sums, from_x
         self.acc, self.sent_c, self.from_c = acc, sent_c, from_c
         self.send_p, self.recv_p, self.send_x, self.recv_x, self.send_c, self.recv_c = sems
 
     def to_p(self, g):
         return copy_to(
-            self.part.at[g, :, 1 - self.p.k], self.pair.at[g], self.send_p.at[g],
+            self.thin.at[g, :, 1 - self.p.k], self.pair.at[g], self.send_p.at[g],
             self.recv_p.at[g], self.p.partner(),
         )
 
@@ -193,7 +194,7 @@
 
     def chip_sum(self, g):
         self.to_p(g).wait_recv()
-        return self.part[g, :, self.p.k] + self.pair[g]
+        return self.part[g, :, self.p.k] + self.pair[g].astype(jnp.float32)
 
     def across_x(self):
         p = self.p
@@ -377,16 +378,19 @@
         def one(i, _):
             g = p.along_x(i)
             at = pl.ds(pl.multiple_of(g * group, LANES), group)
-            scatter.part[g] = jnp.dot(
+            value = jnp.dot(
                 tables[at, :], products[which], preferred_element_type=jnp.float32
             ).reshape(p.nc, 2, rows, levels)
+            scatter.part[g] = value
+            if scatter.thin is not scatter.part:
+                scatter.thin[g] = value.astype(scatter.thin.dtype)
             scatter.to_p(g).start()
             return 0
 
         lax.fori_loop(1, p.nx + 1, one, 0)
 
     crossed = Scatter(p, *cross_buffers)
-    selfed = Scatter(p, *self_buffers)
+    selfed = Scatter(p, self_buffers[0], *self_buffers)
     project(crossed, 0)
     crossed.across_x()
     project(selfed, 1)
@@ -406,9 +410,9 @@
         answer[...] += jnp.where(row == m, full, 0.0)
         return 0
 
-    lax.fori_loop(0, rows // 2, solve, 0)
+    lax.fori_loop(0, rows // 4, solve, 0)
     second.relay_c()
-    lax.fori_loop(rows // 2, rows, solve, 0)
+    lax.fori_loop(rows // 4, rows, solve, 0)
     second.relay_x()
 
     @pl.loop(0, p.nx)
@@ -461,9 +465,14 @@
     gather_sems = [
         dma((groups_x, chips)), dma((chips,)), dma((groups_x, chips)), dma((groups_x, groups_z)),
     ]
+    own_part = pltpu.VMEM((groups_x, chips, 2, rows, levels), wide)
+    cross_first = [
+        own_part,
+        pltpu.VMEM((groups_x, chips, 2, rows, levels), narrow),
+        pltpu.VMEM((groups_x, chips, rows, levels), narrow),
+    ]
+    self_first = [own_part, pltpu.VMEM((groups_x, chips, rows, levels), wide)]
     scatter_buffers = [
-        pltpu.VMEM((groups_x, chips, 2, rows, levels), wide),
-        pltpu.VMEM((groups_x, chips, rows, levels), wide),
         pltpu.VMEM((groups_x, chips, rows, levels), narrow),
         pltpu.VMEM((groups_x, chips, rows, levels), narrow),
         pltpu.VMEM((chips, rows, levels), wide),
@@ -499,8 +508,8 @@
             gather_sems,
             gather_sems,
             gather_sems,
-            scatter_buffers,
-            scatter_buffers,
+            cross_first + scatter_buffers,
+            self_first + scatter_buffers,
         ],
         compiler_params=pltpu.CompilerParams(
             collective_id=0, has_side_effects=True, vmem_limit_bytes=LIMIT_ONE

time: 45.9 us -> 44.7 us (0.974)
  Pallas kernels: 45.1 us -> 43.9 us
    pallas_call x1, Pallas kernels: 42.5 us -> 41.3 us  [on_device(): pl.pallas_call(body, out_shape=(jax.ShapeDtypeStruct((points, levels), wi...]
where the time goes in v6:
time: 44.7 us; the launch traced here: 44.5 us
  Pallas kernels  43.9 us (98%)
  between operations  0.64 us (1%)
    pallas_call x1, Pallas kernels, on_device(): pl.pallas_call(body, out_shape=(jax.ShapeDtypeStruct((points, levels), wi...  41.3 us
    pallas_call x1, Pallas kernels, on_device(): pl.pallas_call(last, out_shape=(jax.ShapeDtypeStruct(high_u.shape, narrow...  2.57 us

profile of v6, /device:TPU:1, one launch (start us, length us, event | category | flops | bytes accessed | tf_op | source)
XLA Modules:
  0.0 44.5 jit_solution(5340162622840933030)
XLA Ops:
  0.6 41.3 %step.1 = (f32[1024,512]{1,0:T(8,128)S(1)}, bf16[1024,512]{1,0:T(8,128)(2,1)S(1)}, bf16[4,8,16,512]{3,2,1,0:T(8,128)(2,1)S(1)}, f32[16,512]{1,0:T(8,128)S(1)}) custom-call(bf16[32,32,512]{2,1,0:T(8,128)(2,1)} %refs_0_.1, bf16[32,32,512]{2,1,0:T(8,128)(2,1)} %refs_1_.1, bf16[16,512]{1,0:T(8,128)(2,1)} %refs_2_.1, bf16[16,512]{1,0:T(8,128)(2,1)} %refs_3_.1, ...), custom_call_target="tpu_custom_call" | custom-call | tf_op jit(solution)/shard_map/step/pallas_call | solution.py:488
  41.9 2.6 %finish.1 = (bf16[32,32,512]{2,1,0:T(8,128)(2,1)}, f32[16,512]{1,0:T(8,128)}) custom-call(f32[1024,512]{1,0:T(8,128)S(1)} %get-tuple-element.6.refs_0_, bf16[1024,512]{1,0:T(8,128)(2,1)S(1)} %get-tuple-element.7.refs_1_, bf16[4,8,16,512]{3,2,1,0:T(8,128)(2,1)S(1)} %get-tuple-element.8.refs_2_, f32[16,512]{1,0:T(8,128)S(1)} %get-tuple-element.9.refs_3_), custom_call_target="tpu_custom_call" | custom-call | tf_op jit(solution)/shard_map/finish/pallas_call | solution.py:532
